TPU v7x, 128 devices: a whole 4x4x4 slice. The times are simulated.
128 devices in a mesh: energy: 8 (over y, core), layer: 16 (over x, z).
Axes of the slice: x: 4, y: 4, z: 4, core: 2. Of those that a mesh axis runs over, the one named last changes fastest.
Arguments:
- correlations: bfloat16 [128, 16, 4, 256, 256], P(('energy', 'layer')), may hold values from -6 to 6
- retarded: bfloat16 [128, 16, 2, 256, 256], P(('energy', 'layer')), may hold values from -0.15625 to 0.15625
- coupling: bfloat16 [16, 256, 256], P('layer'), may hold values from -0.375 to 0.375
- phonon_shifts: int32 [4], replicated, may hold values from 1 to 4, as said below
- phonon_coupling: float32 [4], replicated, may hold values from 0.3 to 1.2
- layer_orbitals: int32 [16], P('layer'), may hold values from 128 to 256, as said below
Outputs:
- left_correlations: bfloat16 [128, 16, 4, 256, 256], P('energy', 'layer')
Inputs may be any that keep to these rules, and one draw needn't show every extreme that they name: `phonon_shifts`: one of the offsets equals 4. `layer_orbitals`: some layer has all 256 orbitals live.
All inputs are finite; a program needn't handle non-finite values.
Results may differ from a plain program's by a relative error of at most 0.025.
Values may be sent and summed in bfloat16 or wider, within the bound.
No kernel may reach another device: no remote copies, remote signals or barrier semaphores. Data moves between devices by JAX's collectives and lax.ppermute only.
A program may use at most 128 MiB of HBM per device.

v0:
```python
import jax
import jax.numpy as jnp
from jax import lax
from jax.sharding import PartitionSpec as P

MODES = 4
SHIFT_MAX = 4
bose_ratio = 0.5


def with_halo(block, sides, width):
    for axis, dim in sides:
        count = lax.axis_size(axis)
        forward = [(i, i + 1) for i in range(count - 1)]
        backward = [(target, source) for source, target in forward]
        low = lax.ppermute(
            lax.slice_in_dim(block, block.shape[dim] - width, None, axis=dim), axis, forward
        )
        high = lax.ppermute(lax.slice_in_dim(block, 0, width, axis=dim), axis, backward)
        block = jnp.concatenate([low, block, high], axis=dim)
    return block


def mode_weights(shift_value):
    occupation = 1.0 / (jnp.exp(bose_ratio * shift_value.astype(jnp.float32)) - 1.0)
    lower_weight = jnp.stack([occupation, occupation, occupation + 1.0, occupation + 1.0])
    upper_weight = jnp.stack([occupation + 1.0, occupation + 1.0, occupation, occupation])
    return (lower_weight, upper_weight)


def left_product(matrix, stacked_block):
    return jnp.einsum(
        "...ab,...kbc->...kac", matrix, stacked_block, preferred_element_type=jnp.float32
    )


def right_product(stacked_block, matrix):
    return jnp.einsum(
        "...kab,...cb->...kac", stacked_block, matrix, preferred_element_type=jnp.float32
    )


def advance(previous, sigma_block, green_block, coupling_block):
    halfway = jnp.einsum(
        "...kab,cb->...kac", previous, coupling_block, preferred_element_type=jnp.float32
    ).astype(jnp.bfloat16)
    spread = jnp.einsum(
        "ab,...kbc->...kac", coupling_block, halfway, preferred_element_type=jnp.float32
    )
    source = (sigma_block.astype(jnp.float32) + spread).astype(jnp.bfloat16)
    green_real = green_block[..., 0, :, :]
    green_imag = green_block[..., 1, :, :]
    source_real = source[..., 0::2, :, :]
    source_imag = source[..., 1::2, :, :]
    inner_real = (
        left_product(green_real, source_real) - left_product(green_imag, source_imag)
    ).astype(jnp.bfloat16)
    inner_imag = (
        left_product(green_real, source_imag) + left_product(green_imag, source_real)
    ).astype(jnp.bfloat16)
    outer_real = right_product(inner_real, green_real) + right_product(inner_imag, green_imag)
    outer_imag = right_product(inner_imag, green_real) - right_product(inner_real, green_imag)
    stacked = jnp.stack([outer_real, outer_imag], axis=-3)
    return stacked.reshape(stacked.shape[:-4] + (4,) + stacked.shape[-2:]).astype(jnp.bfloat16)


def body(correlations, retarded, coupling, phonon_shifts, phonon_coupling, layer_orbitals):
    regrouped = lax.all_to_all(correlations, "layer", split_axis=1, concat_axis=0, tiled=True)
    energies_here = regrouped.shape[0]
    orbital_count = regrouped.shape[-1]
    padded = with_halo(regrouped, (("energy", 0),), SHIFT_MAX)
    accumulated = jnp.zeros(regrouped.shape, jnp.float32)
    for mode_index in range(MODES):
        shift_value = phonon_shifts[mode_index]
        lower_weight, upper_weight = mode_weights(shift_value)
        lower_block = lax.dynamic_slice_in_dim(padded, SHIFT_MAX - shift_value, energies_here, 0)
        upper_block = lax.dynamic_slice_in_dim(padded, SHIFT_MAX + shift_value, energies_here, 0)
        accumulated = accumulated + phonon_coupling[mode_index] * (
            lower_weight[:, None, None] * lower_block.astype(jnp.float32)
            + upper_weight[:, None, None] * upper_block.astype(jnp.float32)
        )
    orbital_index = jnp.arange(orbital_count, dtype=jnp.int32)
    live_count = layer_orbitals[:, None, None, None]
    live_mask = (orbital_index[:, None] < live_count) & (orbital_index[None, :] < live_count)
    sigma_blocks = jnp.where(live_mask, accumulated, 0.0).astype(jnp.bfloat16)
    returned = lax.all_to_all(sigma_blocks, "layer", split_axis=0, concat_axis=1, tiled=True)
    couplings = lax.all_gather(coupling, "layer", axis=0, tiled=True)
    layer_total = returned.shape[1]

    def layer_step(layer_index, state):
        previous, finished = state
        current = advance(
            previous,
            lax.dynamic_index_in_dim(returned, layer_index, 1, keepdims=False),
            lax.dynamic_index_in_dim(retarded, layer_index, 1, keepdims=False),
            lax.dynamic_index_in_dim(couplings, layer_index, 0, keepdims=False),
        )
        finished = lax.dynamic_update_index_in_dim(finished, current, layer_index, 1)
        return (current, finished)

    _, finished = lax.fori_loop(
        0, layer_total, layer_step, (correlations[:, 0], jnp.zeros_like(correlations))
    )
    return lax.all_to_all(finished, "layer", split_axis=1, concat_axis=0, tiled=True)


def solution(mesh):
    return jax.shard_map(
        body,
        mesh=mesh,
        in_specs=(
            P(("energy", "layer"), None, None, None, None),
            P(("energy", "layer"), None, None, None, None),
            P("layer", None, None),
            P(),
            P(),
            P("layer"),
        ),
        out_specs=P("energy", "layer", None, None, None),
        check_vma=False,
    )
```

profile of v0, /device:TPU:8, one launch (start us, length us, event | category | flops | bytes accessed | tf_op | source)
XLA Modules:
  0.0 559.1 jit_solution(11851508432102478930)
XLA Ops:
  6.5 12.2 %copy.25 = bf16[1,16,4,256,256]{3,4,2,0,1:T(8,128)(2,1)} copy(bf16[1,16,4,256,256]{4,3,2,1,0:T(8,128)(2,1)} %param.8) | data formatting | bytes 16777216 | tf_op args[0]
  18.8 104.3 %all_to_all.39 = bf16[1,16,4,256,256]{3,4,2,0,1:T(8,128)(2,1)S(1)} all-to-all(bf16[1,16,4,256,256]{3,4,2,0,1:T(8,128)(2,1)} %copy.25), channel_id=1, replica_groups=mesh['energy'=8,'layer'=16] {'layer'}, dimensions={1} | all-to-all | bytes 16777216 | tf_op jit(solution)/shard_map/all_to_all | solution.py:68
  123.1 1.6 slice_bitcast_fusion.11
  124.7 2.4 copy-done
  128.6 1.9 collective-permute-start.1
  130.6 2.4 collective-permute-start
  148.3 6.1 %collective-permute-done.1 = bf16[4,1,4,256,256]{3,4,2,0,1:T(8,128)(2,1)S(1)} collective-permute-done((bf16[4,1,4,256,256]{3,4,2,0,1:T(8,128)(2,1)}, bf16[4,1,4,256,256]{3,4,2,0,1:T(8,128)(2,1)S(1)}, u32[]{:S(2)}, u32[]{:S(2)}) %collective-permute-start.1) | collective-permute-done | bytes 2097184 | tf_op jit(solution)/shard_map/ppermute | solution.py:19
  154.4 3.8 collective-permute-done
  158.2 6.4 %pad_maximum_fusion = bf16[24,1,4,256,256]{3,4,2,0,1:T(8,128)(2,1)S(1)} fusion(bf16[4,1,4,256,256]{3,4,2,0,1:T(8,128)(2,1)} %copy-done.1, bf16[16,1,4,256,256]{3,4,2,0,1:T(8,128)(2,1)} %bitcast.174, bf16[4,1,4,256,256]{3,4,2,0,1:T(8,128)(2,1)} %collective-permute-done), kind=kLoop, calls=%fused_computation.37 | loop fusion | flops 12582912 | bytes 25165824 | tf_op jit(solution)/shard_map/concatenate | solution.py:20
  164.6 20.0 %fusion.29 = bf16[16,1,4,256,256]{3,4,2,1,0:T(8,128)(2,1)} fusion(bf16[24,1,4,256,256]{3,4,2,0,1:T(8,128)(2,1)S(1)} %pad_maximum_fusion, s32[]{:T(128)S(6)} %select_n.47, f32[4]{0:T(128)S(1)} %get-tuple-element.136, s32[]{:T(128)S(6)} %select_n.46, f32[4]{0:T(128)S(1)} %get-tuple-element.135, f32[]{:T(128)} %bitcast.51, s32[]{:T(128)S(6)} %select_n.45, ...), kind=kLoop, calls=%fused_computation.38 | loop fusion | flops 121634816 | bytes 75563184 | tf_op jit(solution)/shard_map/convert_element_type | solution.py:85
  184.6 4.7 all-to-all-start.1
  191.2 142.2 %all-gather.2.cloned.1.call-done = bf16[16,256,256]{2,1,0:T(8,128)(2,1)} async-done(((bf16[1,256,256]{2,1,0:T(8,128)(2,1)}), bf16[16,256,256]{2,1,0:T(8,128)(2,1)}) %all-gather.2.cloned.1.call-update) | async-done | bytes 2097168 | tf_op jit(solution)/shard_map/all_gather | solution.py:87
  333.4 6.0 %all-to-all-done.1 = bf16[16,1,4,256,256]{3,4,2,1,0:T(8,128)(2,1)} async-done(((bf16[16,1,4,256,256]{3,4,2,1,0:T(8,128)(2,1)}), bf16[16,1,4,256,256]{3,4,2,1,0:T(8,128)(2,1)}, u32[]{:S(2)}, u32[]{:S(2)}) %all-to-all-start.1) | async-done | bytes 8388640 | tf_op jit(solution)/shard_map/all_to_all | solution.py:86
  339.3 92.7 %while.15 = (s32[]{:T(128)}, bf16[1,4,256,256]{3,2,1,0:T(8,128)(2,1)S(1)}, bf16[1,16,4,256,256]{4,3,2,1,0:T(8,128)(2,1)}, bf16[1,16,4,256,256]{3,4,2,1,0:T(8,128...) while((s32[]{:T(128)}, ...), condition=%wide.region_1.2_spmd, body=%wide.region_0.1_spmd.sunk | while | flops 807665664 | bytes 13895261 | solution.py:101
  340.3 1.7 fusion.67
  346.1 1.7 fusion.67
  351.9 1.7 fusion.67
  357.7 1.7 fusion.67
  363.5 1.7 fusion.67
  369.3 1.7 fusion.67
  375.1 1.7 fusion.67
  380.9 1.7 fusion.67
  386.7 1.7 fusion.67
  392.5 1.7 fusion.67
  398.3 1.7 fusion.67
  404.0 1.7 fusion.67
  409.8 1.7 fusion.67
  415.6 1.7 fusion.67
  421.4 1.7 fusion.67
  427.2 1.7 fusion.67
  432.0 112.4 %all_to_all.40 = bf16[1,16,4,256,256]{4,3,2,0,1:T(8,128)(2,1)} all-to-all(bf16[1,16,4,256,256]{4,3,2,0,1:T(8,128)(2,1)} %bitcast.176), channel_id=1, replica_groups=mesh['energy'=8,'layer'=16] {'layer'}, dimensions={1} | all-to-all | bytes 16777216 | tf_op jit(solution)/shard_map/all_to_all | solution.py:104
  544.4 7.8 %copy.49 = bf16[16,1,4,256,256]{4,3,2,1,0:T(8,128)(2,1)} copy(bf16[16,1,4,256,256]{4,3,2,1,0:T(8,128)(2,1)} %bitcast.175) | data formatting | bytes 16777216
  (212 shorter events, 69.3 us)
Async XLA Ops:
  18.8 114.2 %copy-start.2 = (s32[4]{0:T(128)S(1)}, s32[4]{0:T(128)}, u32[]{:S(2)}) copy-start(s32[4]{0:T(128)} %param.11) | copy-start | bytes 52
  18.8 128.8 %copy-start.3 = (f32[4]{0:T(128)S(1)}, f32[4]{0:T(128)}, u32[]{:S(2)}) copy-start(f32[4]{0:T(128)} %param.12) | copy-start | bytes 52
  123.1 4.0 copy-start
  128.6 25.8 %collective-permute-start.1 = (bf16[4,1,4,256,256]{3,4,2,0,1:T(8,128)(2,1)}, bf16[4,1,4,256,256]{3,4,2,0,1:T(8,128)(2,1)S(1)}, u32[]{:S(2)}, u32[]{:S(2)}) collective-permute-start(bf16[4,1,4,256,256]{3,4,2,0,1:T(8,128)(2,1)} %slice_bitcast_fusion.10), channel_id=1, source_target_pairs={{16,0},{32,16},{48,32},{64,48},{80,64},{96,80},{112,96},{17,1},{33... | collective-permute-start | bytes 6291464 | tf_op jit(solution)/shard_map/ppermute | solution.py:19
  130.6 27.7 %collective-permute-start = (bf16[4,1,4,256,256]{3,4,2,0,1:T(8,128)(2,1)}, bf16[4,1,4,256,256]{3,4,2,0,1:T(8,128)(2,1)}, u32[]{:S(2)}, u32[]{:S(2)}) collective-permute-start(bf16[4,1,4,256,256]{3,4,2,0,1:T(8,128)(2,1)} %slice_bitcast_fusion.11), channel_id=1, source_target_pairs={{0,16},{16,32},{32,48},{48,64},{64,80},{80,96},{96,112},{1,17},{17... | collective-permute-start | bytes 6291464 | tf_op jit(solution)/shard_map/ppermute | solution.py:16
  154.4 3.8 copy-start.1
  184.6 154.7 %all-to-all-start.1 = ((bf16[16,1,4,256,256]{3,4,2,1,0:T(8,128)(2,1)}), bf16[16,1,4,256,256]{3,4,2,1,0:T(8,128)(2,1)}, u32[]{:S(2)}, u32[]{:S(2)}) async-start(bf16[16,1,4,256,256]{3,4,2,1,0:T(8,128)(2,1)} %fusion.29), calls=%async_computation.1 | async-start | bytes 16777216 | tf_op jit(solution)/shard_map/all_to_all | solution.py:86
  189.4 144.0 %all-gather.2.cloned.1.call-start = ((), (), s32[]{:S(2)}) async-start(), calls=%async_computation.3 | async-start | bytes 2228224 | tf_op jit(solution)/shard_map/all_gather | solution.py:87
Sparse Core Ops, SparseCore 0:
  192.3 140.9 all-gather.1
where the time goes:
time: 561 us; the launch traced here: 559 us
  blocking collectives  217 us (39%)
  waiting for transfers between devices  159 us (28%)
  matrix products  61.4 us (11%)
  local copies, waits for them, and re-layouts  57.3 us (10%)
  other arithmetic  27.6 us (5%)
  between operations  27 us (5%)
  starting transfers between devices  9.1 us (2%)
    all_gather x1, waiting for transfers between devices, body(): couplings = lax.all_gather(coupling, 'layer', axis=0, tiled=True)  142 us
    all_to_all x1, blocking collectives, body(): lax.all_to_all(finished, 'layer', split_axis=1, concat_axis=0, tiled=True)  112 us
    all_to_all x1, blocking collectives, body(): lax.all_to_all(correlations, 'layer', split_axis=1, concat_axis=0, tiled=...  104 us
    dot_general x16, matrix products, advance(): jnp.einsum('ab,...kbc->...kac', coupling_block, halfway, preferred_elemen...  27.3 us
    unnamed x10, local copies, waits for them, and re-layouts  22.5 us
    convert_element_type x1, other arithmetic, body(): sigma_blocks = jnp.where(live_mask, accumulated, 0.0).astype(jnp.bfloat16)  20 us
    dot_general x64, matrix products, right_product(): jnp.einsum('...kab,...cb->...kac', stacked_block, matrix, preferred_eleme...  17.5 us
    dot_general x64, matrix products, left_product(): jnp.einsum('...ab,...kbc->...kac', matrix, stacked_block, preferred_eleme...  16.5 us
  transfers between devices with their start and end apart: 4, of which 4 were waited for; matrix products, arithmetic and copies ran while one was open for 1% of the time, Pallas kernels for 0%

commit v1 on v0

--- a/solution.py
+++ b/solution.py
@@ -84,7 +84,9 @@
     live_mask = (orbital_index[:, None] < live_count) & (orbital_index[None, :] < live_count)
     sigma_blocks = jnp.where(live_mask, accumulated, 0.0).astype(jnp.bfloat16)
     returned = lax.all_to_all(sigma_blocks, "layer", split_axis=0, concat_axis=1, tiled=True)
-    couplings = lax.all_gather(coupling, "layer", axis=0, tiled=True)
+    couplings = jnp.concatenate(
+        lax.all_to_all(jnp.stack([coupling] * lax.axis_size("layer")), "layer", 0, 0), axis=0
+    )
     layer_total = returned.shape[1]
 
     def layer_step(layer_index, state):

time: 561 us -> 542 us (0.966)
  between operations: 27 us -> 13.6 us
  blocking collectives: 217 us -> 208 us
    all_to_all x1, waiting for transfers between devices: 5.97 us -> 152 us  [body(): lax.all_to_all(sigma_blocks, 'layer', split_axis=0, concat_axis=1, tiled=...]
    all_gather x1 -> x0, waiting for transfers between devices: 142 us -> none  [body(): couplings = lax.all_gather(coupling, 'layer', axis=0, tiled=True)]
    all_to_all x1, blocking collectives: 112 us -> 104 us  [body(): lax.all_to_all(finished, 'layer', split_axis=1, concat_axis=0, tiled=True)]
    ppermute x1, waiting for transfers between devices: 6.13 us -> 0.15 us  [with_halo(): lax.ppermute(lax.slice_in_dim(block, 0, width, axis=dim), axis, backward)]
    unnamed x10 -> x12, local copies, waits for them, and re-layouts: 22.5 us -> 22.5 us
  transfers between devices with their start and end apart: 4 -> 4, of which waited for: 4 -> 3; matrix products, arithmetic and copies ran while one was open for 1% -> 6% of each run, Pallas kernels for 0% -> 0%
where the time goes in v1:
time: 542 us; the launch traced here: 540 us
  blocking collectives  208 us (38%)
  waiting for transfers between devices  156 us (29%)
  matrix products  61.4 us (11%)
  local copies, waits for them, and re-layouts  58.9 us (11%)
  other arithmetic  27.8 us (5%)
  between operations  13.6 us (3%)
  starting transfers between devices  13.5 us (2%)
    all_to_all x1, waiting for transfers between devices, body(): lax.all_to_all(sigma_blocks, 'layer', split_axis=0, concat_axis=1, tiled=...  152 us
    all_to_all x1, blocking collectives, body(): lax.all_to_all(correlations, 'layer', split_axis=1, concat_axis=0, tiled=...  104 us
    all_to_all x1, blocking collectives, body(): lax.all_to_all(finished, 'layer', split_axis=1, concat_axis=0, tiled=True)  104 us
    dot_general x16, matrix products, advance(): jnp.einsum('ab,...kbc->...kac', coupling_block, halfway, preferred_elemen...  27.3 us
    unnamed x12, local copies, waits for them, and re-layouts  22.5 us
    convert_element_type x1, other arithmetic, body(): sigma_blocks = jnp.where(live_mask, accumulated, 0.0).astype(jnp.bfloat16)  20.1 us
    dot_general x64, matrix products, right_product(): jnp.einsum('...kab,...cb->...kac', stacked_block, matrix, preferred_eleme...  17.5 us
    dot_general x64, matrix products, left_product(): jnp.einsum('...ab,...kbc->...kac', matrix, stacked_block, preferred_eleme...  16.5 us
  transfers between devices with their start and end apart: 4, of which 3 were waited for; matrix products, arithmetic and copies ran while one was open for 6% of the time, Pallas kernels for 0%

profile of v1, /device:TPU:8, one launch (start us, length us, event | category | flops | bytes accessed | tf_op | source)
XLA Modules:
  0.0 540.4 jit_solution(3757865576755807672)
XLA Ops:
  0.0 12.2 %copy.25 = bf16[1,16,4,256,256]{3,4,2,0,1:T(8,128)(2,1)} copy(bf16[1,16,4,256,256]{4,3,2,1,0:T(8,128)(2,1)} %param.8) | data formatting | bytes 16777216 | tf_op args[0]
  12.2 104.3 %all_to_all.44 = bf16[1,16,4,256,256]{3,4,2,0,1:T(8,128)(2,1)S(1)} all-to-all(bf16[1,16,4,256,256]{3,4,2,0,1:T(8,128)(2,1)} %copy.25), channel_id=1, replica_groups=mesh['energy'=8,'layer'=16] {'layer'}, dimensions={1} | all-to-all | bytes 16777216 | tf_op jit(solution)/shard_map/all_to_all | solution.py:68
  116.6 1.6 slice_bitcast_fusion.11
  118.2 2.4 copy-done
  122.1 1.9 collective-permute-start.1
  124.0 2.4 collective-permute-start
  126.5 1.5 stack.128
  128.0 4.4 all-to-all-start.2
  147.9 3.8 collective-permute-done
  151.7 6.4 %pad_maximum_fusion = bf16[24,1,4,256,256]{3,4,2,0,1:T(8,128)(2,1)S(1)} fusion(bf16[4,1,4,256,256]{3,4,2,0,1:T(8,128)(2,1)} %copy-done.1, bf16[16,1,4,256,256]{3,4,2,0,1:T(8,128)(2,1)} %bitcast.176, bf16[4,1,4,256,256]{3,4,2,0,1:T(8,128)(2,1)} %collective-permute-done), kind=kLoop, calls=%fused_computation.37 | loop fusion | flops 12582912 | bytes 25165824 | tf_op jit(solution)/shard_map/concatenate | solution.py:20
  158.1 20.1 %fusion.29 = bf16[16,1,4,256,256]{3,4,2,1,0:T(8,128)(2,1)} fusion(bf16[24,1,4,256,256]{3,4,2,0,1:T(8,128)(2,1)S(1)} %pad_maximum_fusion, s32[]{:T(128)S(6)} %select_n.47, f32[4]{0:T(128)S(1)} %get-tuple-element.136, s32[]{:T(128)S(6)} %select_n.46, f32[4]{0:T(128)S(1)} %get-tuple-element.135, f32[]{:T(128)} %bitcast.51, s32[]{:T(128)S(6)} %select_n.45, ...), kind=kLoop, calls=%fused_computation.38 | loop fusion | flops 121634816 | bytes 75563184 | tf_op jit(solution)/shard_map/convert_element_type | solution.py:85
  178.2 4.7 all-to-all-start.1
  184.1 151.9 %all-to-all-done.1 = bf16[16,1,4,256,256]{3,4,2,1,0:T(8,128)(2,1)} async-done(((bf16[16,1,4,256,256]{3,4,2,1,0:T(8,128)(2,1)}), bf16[16,1,4,256,256]{3,4,2,1,0:T(8,128)(2,1)}, u32[]{:S(2)}, u32[]{:S(2)}) %all-to-all-start.1) | async-done | bytes 8388640 | tf_op jit(solution)/shard_map/all_to_all | solution.py:86
  336.0 92.7 %while.15 = (s32[]{:T(128)}, bf16[1,4,256,256]{3,2,1,0:T(8,128)(2,1)S(1)}, bf16[1,16,4,256,256]{4,3,2,1,0:T(8,128)(2,1)}, bf16[1,16,4,256,256]{3,4,2,1,0:T(8,128...) while((s32[]{:T(128)}, ...), condition=%wide.region_1.2_spmd, body=%wide.region_0.1_spmd.sunk | while | flops 807665664 | bytes 13895261 | solution.py:103
  337.0 1.7 fusion.67
  342.8 1.7 fusion.67
  348.6 1.7 fusion.67
  354.4 1.7 fusion.67
  360.1 1.7 fusion.67
  365.9 1.7 fusion.67
  371.7 1.7 fusion.67
  377.5 1.7 fusion.67
  383.3 1.7 fusion.67
  389.1 1.7 fusion.67
  394.9 1.7 fusion.67
  400.7 1.7 fusion.67
  406.5 1.7 fusion.67
  412.3 1.7 fusion.67
  418.1 1.7 fusion.67
  423.9 1.7 fusion.67
  428.7 104.0 %all_to_all.45 = bf16[1,16,4,256,256]{4,3,2,0,1:T(8,128)(2,1)} all-to-all(bf16[1,16,4,256,256]{4,3,2,0,1:T(8,128)(2,1)} %bitcast.178), channel_id=1, replica_groups=mesh['energy'=8,'layer'=16] {'layer'}, dimensions={1} | all-to-all | bytes 16777216 | tf_op jit(solution)/shard_map/all_to_all | solution.py:106
  532.7 7.8 %copy.49 = bf16[16,1,4,256,256]{4,3,2,1,0:T(8,128)(2,1)} copy(bf16[16,1,4,256,256]{4,3,2,1,0:T(8,128)(2,1)} %bitcast.177) | data formatting | bytes 16777216
  (214 shorter events, 68.8 us)
Async XLA Ops:
  12.2 114.2 %copy-start.2 = (bf16[1,256,256]{2,1,0:T(8,128)(2,1)S(1)}, bf16[1,256,256]{2,1,0:T(8,128)(2,1)}, u32[]{:S(2)}) copy-start(bf16[1,256,256]{2,1,0:T(8,128)(2,1)} %param.10) | copy-start | bytes 393220
  12.2 120.2 %copy-start.3 = (s32[4]{0:T(128)S(1)}, s32[4]{0:T(128)}, u32[]{:S(2)}) copy-start(s32[4]{0:T(128)} %param.11) | copy-start | bytes 52
  12.2 134.7 %copy-start.4 = (f32[4]{0:T(128)S(1)}, f32[4]{0:T(128)}, u32[]{:S(2)}) copy-start(f32[4]{0:T(128)} %param.12) | copy-start | bytes 52
  116.6 4.0 copy-start
  122.1 25.8 %collective-permute-start.1 = (bf16[4,1,4,256,256]{3,4,2,0,1:T(8,128)(2,1)}, bf16[4,1,4,256,256]{3,4,2,0,1:T(8,128)(2,1)S(1)}, u32[]{:S(2)}, u32[]{:S(2)}) collective-permute-start(bf16[4,1,4,256,256]{3,4,2,0,1:T(8,128)(2,1)} %slice_bitcast_fusion.10), channel_id=1, source_target_pairs={{16,0},{32,16},{48,32},{64,48},{80,64},{96,80},{112,96},{17,1},{33... | collective-permute-start | bytes 6291464 | tf_op jit(solution)/shard_map/ppermute | solution.py:19
  124.0 27.7 %collective-permute-start = (bf16[4,1,4,256,256]{3,4,2,0,1:T(8,128)(2,1)}, bf16[4,1,4,256,256]{3,4,2,0,1:T(8,128)(2,1)}, u32[]{:S(2)}, u32[]{:S(2)}) collective-permute-start(bf16[4,1,4,256,256]{3,4,2,0,1:T(8,128)(2,1)} %slice_bitcast_fusion.11), channel_id=1, source_target_pairs={{0,16},{16,32},{32,48},{48,64},{64,80},{80,96},{96,112},{1,17},{17... | collective-permute-start | bytes 6291464 | tf_op jit(solution)/shard_map/ppermute | solution.py:16
  128.0 50.2 %all-to-all-start.2 = ((bf16[16,1,256,256]{3,2,1,0:T(8,128)(2,1)}), bf16[16,1,256,256]{3,2,1,0:T(8,128)(2,1)}, u32[]{:S(2)}, u32[]{:S(2)}) async-start(bf16[16,1,256,256]{3,2,1,0:T(8,128)(2,1)} %stack.128), calls=%async_computation.2 | async-start | bytes 4194304 | tf_op jit(solution)/shard_map/all_to_all | solution.py:88
  147.9 3.8 copy-start.1
  178.2 157.8 %all-to-all-start.1 = ((bf16[16,1,4,256,256]{3,4,2,1,0:T(8,128)(2,1)}), bf16[16,1,4,256,256]{3,4,2,1,0:T(8,128)(2,1)}, u32[]{:S(2)}, u32[]{:S(2)}) async-start(bf16[16,1,4,256,256]{3,4,2,1,0:T(8,128)(2,1)} %fusion.29), calls=%async_computation.1 | async-start | bytes 16777216 | tf_op jit(solution)/shard_map/all_to_all | solution.py:86
